TPU v7x, 256 devices: a whole 4x4x8 slice. The times are simulated.
256 devices in a mesh: tm: 16 (over x, z_hi, core), input: 16 (over z_lo, y).
Axes of the slice: x: 4, y: 4, z: 8 (z_hi: 2, z_lo: 4; z = z_hi * 4 + z_lo), core: 2. Of those that a mesh axis runs over, the one named last changes fastest.
Arguments:
- samples: bfloat16 [2, 262144, 2048], P(None, 'tm', 'input'), may hold values from -6 to 6
- filter_taps: float32 [16, 1024], replicated, may hold values from -1.5 to 1.5
Outputs:
- visibilities: bfloat16 [2, 64, 2048, 2048], P(None, 'tm', 'input')
All inputs are finite; a program needn't handle non-finite values.
Results may differ from a plain program's by a relative error of at most 0.0056.
Values may be sent and summed in bfloat16 or wider, within the bound.
A program may use at most 192 MiB of HBM per device.

v0:
```python
import jax
import jax.numpy as jnp
from jax import lax
from jax.sharding import PartitionSpec as P

CH_DEV = 4


def passed_along(shard, axis, by):
    size = lax.axis_size(axis)
    pairs = [(i, i + by) for i in range(size) if 0 <= i + by < size]
    return lax.ppermute(shard, axis, pairs)


def dft_table(count, length):
    chan = jnp.arange(count, dtype=jnp.int32)
    point = jnp.arange(length, dtype=jnp.int32)
    phase = chan[:, None] * point[None, :] % length
    theta = 2.0 * jnp.pi / length * phase.astype(jnp.float32)
    scale = 1.0 / jnp.sqrt(jnp.float32(length))
    cosine = jnp.cos(theta) * scale
    sine = jnp.sin(theta) * scale
    real_rows = jnp.stack([cosine, sine], axis=1)
    imag_rows = jnp.stack([-sine, cosine], axis=1)
    return jnp.concatenate([real_rows, imag_rows], axis=0)


def filter_frames(padded, filter_taps, count):
    filtered = jnp.zeros((2, count, padded.shape[2], padded.shape[3]), jnp.float32)
    for tap in range(filter_taps.shape[0]):
        filtered = filtered + filter_taps[tap][None, None, :, None] * padded[
            :, tap : tap + count
        ].astype(jnp.float32)
    return filtered


def transform(filtered, table):
    spectra = jnp.einsum("kcn,cfna->kfa", table, filtered, precision=lax.Precision.HIGHEST)
    return spectra.reshape(2, table.shape[0] // 2, filtered.shape[1], filtered.shape[3])


def on_device(samples, filter_taps):
    nch = filter_taps.shape[1]
    rim = filter_taps.shape[0] - 1
    width = samples.shape[2]
    frames_here = samples.shape[1] // nch
    local = samples.reshape(2, frames_here, nch, width)
    table = dft_table(CH_DEV * lax.axis_size("tm"), nch)
    ahead = passed_along(local[:, :rim], "tm", -1)
    padded = jnp.concatenate([local, ahead], axis=1)
    spectra = transform(filter_frames(padded, filter_taps, frames_here), table)
    spectra = spectra.astype(jnp.bfloat16)
    turned = lax.all_to_all(spectra, "tm", split_axis=1, concat_axis=2, tiled=True)
    scale = 1.0 / turned.shape[2]
    real_part = turned[0]
    imag_part = turned[1]
    left = jnp.concatenate(
        [
            jnp.concatenate([real_part, imag_part], axis=1),
            jnp.concatenate([imag_part, -real_part], axis=1),
        ],
        axis=2,
    )
    right_block = lax.all_gather(turned, "input", axis=3, tiled=True)
    stacked = jnp.concatenate([right_block[0], right_block[1]], axis=1)
    product = jnp.einsum("cfa,cfb->cab", left, stacked, preferred_element_type=jnp.float32) * scale
    product = product.reshape(product.shape[0], 2, width, right_block.shape[3])
    return jnp.transpose(product, (1, 0, 2, 3)).astype(jnp.bfloat16)


def solution(mesh):
    in_specs = (P(None, "tm", "input"), P())
    out_specs = P(None, "tm", "input", None)
    return jax.shard_map(
        on_device, mesh=mesh, in_specs=in_specs, out_specs=out_specs, check_vma=False
    )
```

profile of v0, /device:TPU:2, one launch (start us, length us, event | category | flops | bytes accessed | tf_op | source)
XLA Modules:
  0.0 423.6 jit_solution(3179844550799687338)
XLA Ops:
  6.5 0.0 copy-start
  6.5 0.0 all-gather.2.cloned.1.call-start
  6.5 4.1 slice.146
  10.6 4.0 copy.51
  14.6 8.5 %collective-permute-start = (bf16[2,15,1024,128]{3,2,0,1:T(8,128)(2,1)}, bf16[2,15,1024,128]{3,2,0,1:T(8,128)(2,1)}, u32[]{:S(2)}, u32[]{:S(2)}) collective-permute-start(bf16[2,15,1024,128]{3,2,0,1:T(8,128)(2,1)} %copy.51), channel_id=1, source_target_pairs={{16,0},{32,16},{48,32},{64,48},{80,64},{96,80},{112,96},{128,112},... | collective-permute-start | bytes 23592968 | tf_op jit(solution)/shard_map/ppermute | solution.py:12
  23.1 1.0 fusion.110
  24.1 1.0 sine_multiply_fusion
  25.1 0.0 copy-done
  25.2 7.5 %constant_dynamic-update-slice_fusion.1 = bf16[2,31,1024,128]{3,2,0,1:T(8,128)(2,1)} fusion(bf16[2,16,1024,128]{3,2,1,0:T(8,128)(2,1)} %bitcast.48), kind=kLoop, calls=%fused_computation.116 | loop fusion | bytes 16777216
  32.7 160.2 %collective-permute-done = bf16[2,15,1024,128]{3,2,0,1:T(8,128)(2,1)} collective-permute-done((bf16[2,15,1024,128]{3,2,0,1:T(8,128)(2,1)}, bf16[2,15,1024,128]{3,2,0,1:T(8,128)(2,1)}, u32[]{:S(2)}, u32[]{:S(2)}) %collective-permute-start) | collective-permute-done | bytes 7864352 | tf_op jit(solution)/shard_map/ppermute | solution.py:12
  192.9 7.1 %constant_dynamic-update-slice_fusion = bf16[2,31,1024,128]{3,2,0,1:T(8,128)(2,1)} fusion(bf16[2,31,1024,128]{3,2,0,1:T(8,128)(2,1)} %constant_dynamic-update-slice_fusion.1, bf16[2,15,1024,128]{3,2,0,1:T(8,128)(2,1)} %collective-permute-done), kind=kLoop, calls=%fused_computation.115 | loop fusion | bytes 15728640 | tf_op jit(solution)/shard_map/concatenate | solution.py:50
  200.1 46.7 %fusion.119 = f32[2,16,1024,128]{3,2,0,1:T(8,128)S(1)} fusion(bf16[2,31,1024,128]{3,2,0,1:T(8,128)(2,1)} %constant_dynamic-update-slice_fusion, f32[1024]{0:T(1024)S(1)} %bitcast.71, f32[1024]{0:T(1024)S(1)} %bitcast.72, f32[1024]{0:T(1024)S(1)} %bitcast.58, f32[1024]{0:T(1024)S(1)} %bitcast.59, f32[1024]{0:T(1024)S(1)} %bitcast.60, ...), kind=kLoop, calls=%fused_computation.1.clone.clone.clone.clone.clone.2 | loop fusion | flops 197132288 | bytes 151060480 | tf_op jit(solution)/shard_map/kcn,cfna->kfa/dot_general | solution.py:38
  246.8 8.9 %fusion.88 = bf16[128,16,128]{2,0,1:T(8,128)(2,1)S(1)} fusion(f32[64,1,1024]{2,0,1:T(8,128)S(1)} %get-tuple-element.26, f32[64,1,1024]{2,0,1:T(8,128)S(1)} %fusion.110, f32[64,1,1024]{2,0,1:T(8,128)S(1)} %get-tuple-element.25, f32[2,16,1024,128]{3,2,0,1:T(8,128)S(1)} %fusion.119), kind=kOutput, calls=%fused_computation.88 | convolution fusion | flops 6443499520 | bytes 18087936 | tf_op jit(solution)/shard_map/kcn,cfna->kfa/dot_general | solution.py:38
  255.7 0.3 copy.33
  256.0 26.1 %all_to_all.18 = bf16[2,64,16,128]{3,2,0,1:T(8,128)(2,1)S(1)} all-to-all(bf16[2,64,16,128]{3,2,0,1:T(8,128)(2,1)S(1)} %copy.33), channel_id=1, replica_groups=mesh['tm'=16,'input'=16] {'tm'}, dimensions={1} | all-to-all | bytes 1048576 | tf_op jit(solution)/shard_map/all_to_all | solution.py:53
  282.1 0.8 copy.41
  282.9 0.0 all-gather.2.cloned.1.call-update
  283.1 0.1 copy.37
  283.3 0.1 copy.38
  283.5 124.6 %all-gather.2.cloned.1.call-done = bf16[2,4,256,2048]{3,2,1,0:T(8,128)(2,1)} async-done(((bf16[2,4,256,128]{3,2,1,0:T(8,128)(2,1)}), bf16[2,4,256,2048]{3,2,1,0:T(8,128)(2,1)}) %all-gather.2.cloned.1.call-update) | async-done | bytes 8388624 | tf_op jit(solution)/shard_map/all_gather | solution.py:64
  408.0 3.8 slice_bitcast_fusion.1
  411.8 2.6 multiply_convert_fusion
  414.5 2.3 copy.56
  (6 shorter events, 0.2 us)
Async XLA Ops:
  6.5 18.6 %copy-start = (f32[16,1024]{1,0:T(8,128)S(1)}, f32[16,1024]{1,0:T(8,128)}, u32[]{:S(2)}) copy-start(f32[16,1024]{1,0:T(8,128)} %param.3) | copy-start | bytes 196612
  6.5 401.5 %all-gather.2.cloned.1.call-start = ((), (), s32[]{:S(2)}) async-start(), calls=%async_computation.1 | async-start | bytes 8912896 | tf_op jit(solution)/shard_map/all_gather | solution.py:64
  14.6 178.3 %collective-permute-start = (bf16[2,15,1024,128]{3,2,0,1:T(8,128)(2,1)}, bf16[2,15,1024,128]{3,2,0,1:T(8,128)(2,1)}, u32[]{:S(2)}, u32[]{:S(2)}) collective-permute-start(bf16[2,15,1024,128]{3,2,0,1:T(8,128)(2,1)} %copy.51), channel_id=1, source_target_pairs={{16,0},{32,16},{48,32},{64,48},{80,64},{96,80},{112,96},{128,112},... | collective-permute-start | bytes 23592968 | tf_op jit(solution)/shard_map/ppermute | solution.py:12
Sparse Core Ops, SparseCore 0:
  283.1 124.8 all-gather.1
where the time goes:
time: 425 us; the launch traced here: 424 us
  waiting for transfers between devices  285 us (67%)
  other arithmetic  48.8 us (11%)
  local copies, waits for them, and re-layouts  30.4 us (7%)
  blocking collectives  26.1 us (6%)
  between operations  13.5 us (3%)
  matrix products  11.5 us (3%)
  starting transfers between devices  8.5 us (2%)
    ppermute x1, waiting for transfers between devices, passed_along(): return lax.ppermute(shard, axis, pairs)  160 us
    all_gather x1, waiting for transfers between devices, on_device(): right_block = lax.all_gather(turned, 'input', axis=3, tiled=True)  125 us
    dot_general x1, other arithmetic, transform(): jnp.einsum('kcn,cfna->kfa', table, filtered, precision=lax.Precision.HIGH...  46.7 us
    all_to_all x1, blocking collectives, on_device(): lax.all_to_all(spectra, 'tm', split_axis=1, concat_axis=2, tiled=True)  26.1 us
    unnamed x4, local copies, waits for them, and re-layouts  11.5 us
    dot_general x1, matrix products, transform(): jnp.einsum('kcn,cfna->kfa', table, filtered, precision=lax.Precision.HIGH...  8.9 us
  transfers between devices with their start and end apart: 2, of which 2 were waited for; matrix products, arithmetic and copies ran while one was open for 2% of the time, Pallas kernels for 0%

commit v1 on v0

v1 whole, which is shorter than its diff:
```python
import functools

import jax
import jax.numpy as jnp
import numpy as np
from jax import lax
from jax.experimental import pallas as pl
from jax.experimental.pallas import tpu as pltpu
from jax.sharding import PartitionSpec as P

MESH = pl.DeviceIdType.MESH
CH_DEV = 4
TM = 16
NY = 4
NZ = 4
INP = NY * NZ


def trig_table(nch):
    chan = CH_DEV * np.arange(TM)[None, :] + np.arange(CH_DEV)[:, None]
    phase = chan[:, :, None] * np.arange(nch)[None, None, :] % nch
    theta = 2.0 * np.pi / nch * phase
    scale = 1.0 / np.sqrt(nch)
    return np.stack([np.cos(theta) * scale, np.sin(theta) * scale]).astype(np.float32)


def kernel(x_hbm, taps_ref, trig_ref, out_hbm, xv, ghi, glo, acc, part, recv, blocks, lt, vout,
           x_sem, turn_send, turn_recv, z_send, z_recv, y_send, y_recv, f_send, f_recv, out_sem):
    t = lax.axis_index("tm")
    i = lax.axis_index("input")
    z = i // NY
    y = lax.rem(i, NY)
    up = lax.rem(y + 1, NY)
    down = lax.rem(y + NY - 1, NY)
    ntaps, nch = taps_ref.shape
    frames = xv.shape[1]
    width = xv.shape[3]
    rows = 2 * TM
    pairs = frames // 2

    def x_copy(p):
        sl = pl.ds(2 * p, 2)
        return pltpu.make_async_copy(x_hbm.at[:, sl], xv.at[:, sl], x_sem.at[p])

    for p in range(pairs):
        x_copy(p).start()

    barrier = pltpu.get_barrier_semaphore()

    @pl.loop(1, TM)
    def _(d):
        pl.semaphore_signal(barrier, inc=1, device_id={"tm": lax.rem(t + d, TM), "input": i}, device_id_type=MESH)

    for d in range(1, NZ):
        pl.semaphore_signal(
            barrier, inc=1, device_id={"tm": t, "input": lax.rem(z + d, NZ) * NY + y}, device_id_type=MESH)
    for side in (up, down):
        pl.semaphore_signal(barrier, inc=1, device_id={"tm": t, "input": z * NY + side}, device_id_type=MESH)

    def weights(c):
        cosine = trig_ref[0, c]
        sine = trig_ref[1, c]

        @pl.loop(0, ntaps)
        def _(tap):
            h = taps_ref[pl.ds(tap, 1), :]
            co = cosine * h
            si = sine * h
            for r0, c0, val in ((0, 0, co), (0, nch, si), (TM, 0, -si), (TM, nch, co)):
                at = pl.multiple_of(tap * rows + r0, TM)
                hi = val.astype(jnp.bfloat16)
                ghi[pl.ds(at, TM), c0:c0 + nch] = hi
                glo[pl.ds(at, TM), c0:c0 + nch] = (val - hi.astype(jnp.float32)).astype(jnp.bfloat16)

        acc[...] = jnp.zeros_like(acc)

    def filtered(c, lo, hi):
        @pl.loop(lo, hi)
        def _(p):
            if c == 0:
                x_copy(p).wait()
            b0 = jnp.concatenate([xv[0, 2 * p], xv[0, 2 * p + 1]], axis=1)
            b1 = jnp.concatenate([xv[1, 2 * p], xv[1, 2 * p + 1]], axis=1)
            both = jnp.concatenate([b0, b1], axis=0)
            prod = jnp.dot(ghi[...], both, preferred_element_type=jnp.float32)
            prod = prod + jnp.dot(glo[...], both, preferred_element_type=jnp.float32)
            for tap in range(ntaps):
                for j in range(2):
                    at = pl.ds(pl.multiple_of((2 * p + j - tap + frames) * rows, rows), rows)
                    acc[at, :] += prod[tap * rows:(tap + 1) * rows, j * width:(j + 1) * width]

    def finish(c):
        for part_index in range(2):
            for owner in range(TM):
                r = part_index * TM + owner
                part[c, owner, part_index] = acc[pl.ds(r, rows, stride=rows), :].astype(jnp.bfloat16)
        recv[c, t] = part[c, t]

    def turn_copy(c, d):
        owner = lax.rem(t + d, TM)
        return pltpu.make_async_remote_copy(
            src_ref=part.at[c, owner], dst_ref=recv.at[c, t],
            send_sem=turn_send.at[c, d], recv_sem=turn_recv.at[c, d],
            device_id={"tm": owner, "input": i}, device_id_type=MESH)

    def turn_start(c):
        @pl.loop(1, TM)
        def _(d):
            turn_copy(c, d).start()

    def z_copy(c, d):
        return pltpu.make_async_remote_copy(
            src_ref=blocks.at[c, i], dst_ref=blocks.at[c, i],
            send_sem=z_send.at[c, d], recv_sem=z_recv.at[c, d],
            device_id={"tm": t, "input": lax.rem(z + d, NZ) * NY + y}, device_id_type=MESH)

    def y_copy(c, d, side):
        slot = lax.rem(z + NZ - d, NZ) * NY + y
        return pltpu.make_async_remote_copy(
            src_ref=blocks.at[c, slot], dst_ref=blocks.at[c, slot],
            send_sem=y_send.at[c, side, d], recv_sem=y_recv.at[c, side, d],
            device_id={"tm": t, "input": z * NY + (up, down)[side]}, device_id_type=MESH)

    def f_copy(c, d, side):
        slot = lax.rem(z + NZ - d, NZ) * NY + (down, up)[side]
        return pltpu.make_async_remote_copy(
            src_ref=blocks.at[c, slot, side], dst_ref=blocks.at[c, slot, side],
            send_sem=f_send.at[c, side, d], recv_sem=f_recv.at[c, side, d],
            device_id={"tm": t, "input": z * NY + (up, down)[side]}, device_id_type=MESH)

    def assemble(c):
        @pl.loop(1, TM)
        def _(d):
            turn_copy(c, d).wait_recv()

        for s in range(TM):
            for h in range(2):
                own = recv[c, s, h, frames:, :]
                if s + 1 < TM:
                    ahead = recv[c, s + 1, h, :frames, :]
                    own = (own.astype(jnp.float32) + ahead.astype(jnp.float32)).astype(jnp.bfloat16)
                blocks[c, i, h, s * frames:(s + 1) * frames, :] = own
        for side in range(2):
            y_copy(c, 0, side).start()
        for d in range(1, NZ):
            z_copy(c, d).start()

    def spread(c):
        for d in range(1, NZ):
            z_copy(c, d).wait_recv()
            for side in range(2):
                y_copy(c, d, side).start()

    def forward(c):
        for d in range(NZ):
            for side in range(2):
                y_copy(c, d, side).wait_recv()
                f_copy(c, d, side).start()

    def correlate(c):
        for d in range(NZ):
            for side in range(2):
                f_copy(c, d, side).wait_recv()
        re = blocks[c, i, 0].T
        im = blocks[c, i, 1].T
        span = re.shape[1]
        lt[:width, :span] = re
        lt[:width, span:] = im
        lt[width:, :span] = im
        lt[width:, span:] = -re

        @pl.loop(0, INP // 2)
        def _(q):
            left = blocks[c, 2 * q].reshape(2 * span, width)
            right = blocks[c, 2 * q + 1].reshape(2 * span, width)
            prod = jnp.dot(lt[...], jnp.concatenate([left, right], axis=1), preferred_element_type=jnp.float32)
            prod = (prod * (1.0 / span)).astype(jnp.bfloat16)
            at = pl.ds(pl.multiple_of(q * 2 * width, 2 * width), 2 * width)
            vout[c, 0, :, at] = prod[:width]
            vout[c, 1, :, at] = prod[width:]

        pltpu.make_async_copy(vout.at[c], out_hbm.at[:, c], out_sem.at[c]).start()

    half = pairs // 2
    weights(0)
    filtered(0, 0, pairs)
    finish(0)
    pl.semaphore_wait(barrier, TM - 1 + NZ - 1 + 2)
    turn_start(0)
    for c in range(1, CH_DEV):
        weights(c)
        filtered(c, 0, half)
        assemble(c - 1)
        filtered(c, half, pairs)
        finish(c)
        turn_start(c)
        spread(c - 1)
        if c >= 2:
            forward(c - 2)
    assemble(CH_DEV - 1)
    spread(CH_DEV - 1)
    for c in range(CH_DEV - 2):
        correlate(c)
    forward(CH_DEV - 2)
    forward(CH_DEV - 1)
    correlate(CH_DEV - 2)
    correlate(CH_DEV - 1)
    for c in range(CH_DEV):
        @pl.loop(1, TM)
        def _(d):
            turn_copy(c, d).wait_send()

        for d in range(1, NZ):
            z_copy(c, d).wait_send()
        for d in range(NZ):
            for side in range(2):
                y_copy(c, d, side).wait_send()
                f_copy(c, d, side).wait_send()
        pltpu.make_async_copy(vout.at[c], out_hbm.at[:, c], out_sem.at[c]).wait()


def on_device(samples, filter_taps):
    ntaps, nch = filter_taps.shape
    width = samples.shape[2]
    frames = samples.shape[1] // nch
    total = frames * TM
    rows = 2 * TM
    local = samples.reshape(2, frames, nch, width)
    dma = pltpu.SemaphoreType.DMA
    return pl.pallas_call(
        kernel,
        out_shape=jax.ShapeDtypeStruct((2, CH_DEV, width, INP * width), jnp.bfloat16),
        in_specs=[
            pl.BlockSpec(memory_space=pl.ANY),
            pl.BlockSpec(memory_space=pltpu.VMEM),
            pl.BlockSpec(memory_space=pltpu.VMEM),
        ],
        out_specs=pl.BlockSpec(memory_space=pl.ANY),
        scratch_shapes=[
            pltpu.VMEM((2, frames, nch, width), jnp.bfloat16),
            pltpu.VMEM((ntaps * rows, 2 * nch), jnp.bfloat16),
            pltpu.VMEM((ntaps * rows, 2 * nch), jnp.bfloat16),
            pltpu.VMEM((2 * frames * rows, width), jnp.float32),
            pltpu.VMEM((CH_DEV, TM, 2, 2 * frames, width), jnp.bfloat16),
            pltpu.VMEM((CH_DEV, TM, 2, 2 * frames, width), jnp.bfloat16),
            pltpu.VMEM((CH_DEV, INP, 2, total, width), jnp.bfloat16),
            pltpu.VMEM((2 * width, 2 * total), jnp.bfloat16),
            pltpu.VMEM((CH_DEV, 2, width, INP * width), jnp.bfloat16),
            dma((frames // 2,)),
            dma((CH_DEV, TM)),
            dma((CH_DEV, TM)),
            dma((CH_DEV, NZ)),
            dma((CH_DEV, NZ)),
            dma((CH_DEV, 2, NZ)),
            dma((CH_DEV, 2, NZ)),
            dma((CH_DEV, 2, NZ)),
            dma((CH_DEV, 2, NZ)),
            dma((CH_DEV,)),
        ],
        compiler_params=pltpu.CompilerParams(
            collective_id=0, has_side_effects=True, vmem_limit_bytes=60 * 1024 * 1024),
        name="correlator",
    )(local, filter_taps, jnp.asarray(trig_table(nch)))


def solution(mesh):
    in_specs = (P(None, "tm", "input"), P())
    out_specs = P(None, "tm", "input", None)
    return jax.shard_map(
        on_device, mesh=mesh, in_specs=in_specs, out_specs=out_specs, check_vma=False
    )
```

time: 425 us -> 135 us (0.32)
  the two profiles are of different devices: /device:TPU:2 before, /device:TPU:96 now
where the time goes in v1:
time: 135 us
  Pallas kernels  130 us (96%)
  local copies, waits for them, and re-layouts  4.79 us (4%)
    pallas_call x1, Pallas kernels, on_device(): pl.pallas_call(kernel, out_shape=jax.ShapeDtypeStruct((2, CH_DEV, width,...  130 us
    unnamed x1, local copies, waits for them, and re-layouts  4.79 us

profile of v1, /device:TPU:96, one launch (start us, length us, event | category | flops | bytes accessed | tf_op | source)
XLA Modules:
  0.0 134.8 jit_solution(18186187730043484502)
XLA Ops:
  0.0 130.0 %correlator.1 = bf16[2,4,128,2048]{3,2,1,0:T(8,128)(2,1)} custom-call(bf16[2,16,1024,128]{3,2,1,0:T(8,128)(2,1)} %bitcast.1, f32[16,1024]{1,0:T(8,128)} %taps_ref.1, f32[2,4,16,1024]{3,2,1,0:T(8,128)} %constant.2.clone.trig_ref), custom_call_target="tpu_custom_call" | custom-call | tf_op jit(solution)/shard_map/correlator/pallas_call | solution.py:230
  130.0 4.8 %copy.5 = bf16[2,4,128,2048]{3,2,1,0:T(8,128)(2,1)} copy(bf16[2,4,128,2048]{3,2,1,0:T(8,128)(2,1)} %correlator.1) | data formatting | bytes 8388608

commit v2 on v1

v2 whole, which is shorter than its diff:
```python
import functools

import jax
import jax.numpy as jnp
import numpy as np
from jax import lax
from jax.experimental import pallas as pl
from jax.experimental.pallas import tpu as pltpu
from jax.sharding import PartitionSpec as P

MESH = pl.DeviceIdType.MESH
CH_DEV = 4
TM = 16
NY = 4
NZ = 4
INP = NY * NZ
GROUP = 8


def trig_table(nch):
    chan = CH_DEV * np.arange(TM)[None, :] + np.arange(CH_DEV)[:, None]
    phase = chan[:, :, None] * np.arange(nch)[None, None, :] % nch
    theta = 2.0 * np.pi / nch * phase
    scale = 1.0 / np.sqrt(nch)
    return np.stack([np.cos(theta) * scale, np.sin(theta) * scale]).astype(np.float32)


def kernel(x_hbm, taps_ref, trig_ref, out_hbm, xv, ghi, acc, part, recv, mid, ahead, merged, crossed, blocks, lt, vout, vsend, vin,
           x_sem, turn_send, turn_recv, mid_send, mid_recv, ahead_send, ahead_recv, cross_send, cross_recv,
           z_send, z_recv, zf_send, y_send, y_recv, b_send, b_recv, v_send, v_recv, out_sem):
    t = lax.axis_index("tm")
    i = lax.axis_index("input")
    x = t // 4
    zhi = lax.rem(t // 2, 2)
    core = lax.rem(t, 2)
    other = 1 - zhi
    z = i // NY
    y = lax.rem(i, NY)
    q = 2 * x + core
    ring = zhi * NZ + z
    toward = jnp.where(x == 0, 1, -1)
    up = lax.rem(y + 1, NY)
    down = lax.rem(y + NY - 1, NY)
    ntaps, nch = taps_ref.shape
    frames = xv.shape[1]
    width = xv.shape[3]
    rows = 2 * TM
    pairs = frames // 2

    def at_ring(member, place):
        place = lax.rem(place + 2 * NZ, 2 * NZ)
        return {"tm": (member // 2) * 4 + 2 * (place // NZ) + lax.rem(member, 2), "input": lax.rem(place, NZ) * NY + y}

    def at_group(member):
        return at_ring(member, ring)

    def at_z(place):
        return {"tm": t, "input": place * NY + y}

    def at_y(place):
        return {"tm": t, "input": z * NY + place}

    def x_copy(p):
        sl = pl.ds(2 * p, 2)
        return pltpu.make_async_copy(x_hbm.at[:, sl], xv.at[:, sl], x_sem.at[p])

    for p in range(pairs):
        x_copy(p).start()

    barrier = pltpu.get_barrier_semaphore()
    peers = [at_group(lax.rem(q + d, GROUP)) for d in range(1, GROUP)]
    peers += [at_ring(q, ring + step) for step in (3, -3)]
    peers += [at_z(lax.rem(z + d, NZ)) for d in range(1, NZ)]
    peers += [at_y(up), at_y(down)]
    for peer in peers:
        pl.semaphore_signal(barrier, inc=1, device_id=peer, device_id_type=MESH)
    steps = (1, -1, NZ)

    @pl.loop(0, GROUP)
    def _(member):
        for step in steps:
            pl.semaphore_signal(barrier, inc=1, device_id=at_ring(member, ring + step), device_id_type=MESH)

    def weights(c):
        cosine = trig_ref[0, c]
        sine = trig_ref[1, c]

        @pl.loop(0, ntaps)
        def _(tap):
            h = taps_ref[pl.ds(tap, 1), :]
            co = cosine * h
            si = sine * h
            for r0, c0, val in ((0, 0, co), (0, nch, si), (TM, 0, -si), (TM, nch, co)):
                at = pl.multiple_of(tap * rows + r0, TM)
                ghi[pl.ds(at, TM), c0:c0 + nch] = val.astype(jnp.bfloat16)

        acc[...] = jnp.zeros_like(acc)

    def filtered(c, lo, hi):
        @pl.loop(lo, hi)
        def _(p):
            if c == 0:
                x_copy(p).wait()
            b0 = jnp.concatenate([xv[0, 2 * p], xv[0, 2 * p + 1]], axis=1)
            b1 = jnp.concatenate([xv[1, 2 * p], xv[1, 2 * p + 1]], axis=1)
            both = jnp.concatenate([b0, b1], axis=0)
            prod = jnp.dot(ghi[...], both, preferred_element_type=jnp.float32)
            for tap in range(ntaps):
                for j in range(2):
                    at = pl.ds(pl.multiple_of((2 * p + j - tap + frames) * rows, rows), rows)
                    acc[at, :] += prod[tap * rows:(tap + 1) * rows, j * width:(j + 1) * width]

    def turn_copy(c, d):
        member = lax.rem(q + d, GROUP)
        return pltpu.make_async_remote_copy(
            src_ref=part.at[c, member, zhi], dst_ref=recv.at[c, q],
            send_sem=turn_send.at[c, d], recv_sem=turn_recv.at[c, d],
            device_id=at_group(member), device_id_type=MESH)

    def mid_copy(c, d):
        member = lax.rem(q + d, GROUP)
        return pltpu.make_async_remote_copy(
            src_ref=part.at[c, member, other], dst_ref=mid.at[c, q],
            send_sem=mid_send.at[c, d], recv_sem=mid_recv.at[c, d],
            device_id=at_ring(member, ring + toward), device_id_type=MESH)

    def ahead_copy(c, member):
        return pltpu.make_async_remote_copy(
            src_ref=part.at[c, member, other, :, pl.ds(0, frames)], dst_ref=ahead.at[c, x],
            send_sem=ahead_send.at[c, member], recv_sem=ahead_recv.at[c, x],
            device_id=at_ring(member, ring + NZ), device_id_type=MESH)

    def ahead_arrival(c, k):
        return pltpu.make_async_remote_copy(
            src_ref=part.at[c, 0, 0, :, pl.ds(0, frames)], dst_ref=ahead.at[c, k],
            send_sem=ahead_send.at[c, 0], recv_sem=ahead_recv.at[c, k],
            device_id=at_ring(q, ring + NZ), device_id_type=MESH)

    def cross_copy(c, side):
        sl = (pl.ds(0, 1), pl.ds(1, 3))[side]
        return pltpu.make_async_remote_copy(
            src_ref=merged.at[c, sl], dst_ref=crossed.at[c, sl],
            send_sem=cross_send.at[c, side], recv_sem=cross_recv.at[c, side],
            device_id=at_ring(q, ring + (3, -3)[side]), device_id_type=MESH)

    def finish(c):
        for h in range(2):
            for owner in range(TM):
                r = h * TM + owner
                member, side = (owner // 4) * 2 + owner % 2, (owner // 2) % 2
                part[c, member, side, h] = acc[pl.ds(r, rows, stride=rows), :].astype(jnp.bfloat16)
        recv[c, q] = part[c, q, zhi]

        @pl.when(core == 0)
        def _():
            for member in range(GROUP):
                ahead_copy(c, member).start()

        for d in range(GROUP):
            mid_copy(c, d).start()
        for d in range(1, GROUP):
            turn_copy(c, d).start()

    def segments(c, slot, stage):
        return blocks.at[c, slot, pl.ds(2 * stage, 2)]

    def z_copy(c, d, stage):
        ref = segments(c, i, stage)
        return pltpu.make_async_remote_copy(
            src_ref=ref, dst_ref=ref,
            send_sem=z_send.at[c, d, stage], recv_sem=z_recv.at[c, d, stage],
            device_id=at_z(lax.rem(z + d, NZ)), device_id_type=MESH)

    def z_far(d):
        return (z == 3) if d == 1 else (z == 0) if d == 3 else None

    def z_each(d, act):
        far = z_far(d)
        if far is None:
            act()
        else:
            pl.when(jnp.logical_not(far))(act)

    inner = jnp.logical_or(z == 1, z == 2)

    def zf_copy(c, stage):
        source = lax.rem(z + 2, NZ)
        target = jnp.where(z == 1, 0, 3)
        ref = segments(c, source * NY + y, stage)
        return pltpu.make_async_remote_copy(
            src_ref=ref, dst_ref=ref,
            send_sem=zf_send.at[c, stage], recv_sem=z_recv.at[c, jnp.where(z == 1, 1, 3), stage],
            device_id=at_z(target), device_id_type=MESH)

    def fwd(c):
        return (up, down)[c % 2]

    def back(c):
        return (down, up)[c % 2]

    def y_copy(c, d, stage):
        ref = segments(c, lax.rem(z + NZ - d, NZ) * NY + y, stage)
        return pltpu.make_async_remote_copy(
            src_ref=ref, dst_ref=ref,
            send_sem=y_send.at[c, d, stage], recv_sem=y_recv.at[c, d, stage],
            device_id=at_y(fwd(c)), device_id_type=MESH)

    def b_copy(c, stage):
        ref = segments(c, i, stage)
        return pltpu.make_async_remote_copy(
            src_ref=ref, dst_ref=ref,
            send_sem=b_send.at[c, stage], recv_sem=b_recv.at[c, stage],
            device_id=at_y(back(c)), device_id_type=MESH)

    def v_copy(c, side):
        return pltpu.make_async_remote_copy(
            src_ref=vsend.at[c, side], dst_ref=vin.at[c, side],
            send_sem=v_send.at[c, side], recv_sem=v_recv.at[c, side],
            device_id=at_y((back(c), fwd(c))[side]), device_id_type=MESH)

    def total(a, b):
        return (a.astype(jnp.float32) + b.astype(jnp.float32)).astype(jnp.bfloat16)

    def send_own(c, stage):
        y_copy(c, 0, stage).start()
        b_copy(c, stage).start()
        for d in (2, 1, 3):
            z_each(d, lambda: z_copy(c, d, stage).start())

    def first_half(c):
        for d in range(GROUP):
            mid_copy(c, d).wait_recv()
        for k in range(4):
            for h in range(2):
                merged[c, k, 0, h] = total(mid[c, 2 * k, h, frames:, :], mid[c, 2 * k + 1, h, :frames, :])
                merged[c, k, 1, h] = mid[c, 2 * k + 1, h, frames:, :]
        for side in range(2):
            cross_copy(c, side).start()
        for d in range(1, GROUP):
            turn_copy(c, d).wait_recv()
        for k in range(4):
            ahead_arrival(c, k).wait_recv()
        for k in range(4):
            there = jnp.minimum(k + zhi, 3)
            for h in range(2):
                at = slice(k * frames, (k + 1) * frames)
                blocks[c, i, 0, h, at] = total(recv[c, 2 * k, h, frames:, :], recv[c, 2 * k + 1, h, :frames, :])
                rest = ahead[c, there, h].astype(jnp.float32)
                if k == 3:
                    rest = jnp.where(zhi == 0, rest, 0.0)
                blocks[c, i, 1, h, at] = total(recv[c, 2 * k + 1, h, frames:, :], rest)
        send_own(c, 0)

    def second_half(c):
        for side in range(2):
            cross_copy(c, side).wait_recv()
        for k in range(4):
            here = jnp.minimum(k + other, 3)
            for h in range(2):
                at = slice(k * frames, (k + 1) * frames)
                blocks[c, i, 2, h, at] = crossed[c, k, 0, h]
                rest = recv[c, 2 * here, h, :frames, :].astype(jnp.float32)
                if k == 3:
                    rest = jnp.where(zhi == 1, rest, 0.0)
                blocks[c, i, 3, h, at] = total(crossed[c, k, 1, h], rest)
        send_own(c, 1)

    def spread(c, stage):
        for d in (2, 1, 3):
            z_copy(c, d, stage).wait_recv()
            if d == 2:
                pl.when(inner)(lambda: zf_copy(c, stage).start())
            y_copy(c, d, stage).start()

    def left_rows(c, slot):
        span = 2 * blocks.shape[4]
        for seg in range(4):
            re = blocks[c, slot, seg, 0]
            im = blocks[c, slot, seg, 1]
            lt[:width, seg * span:(seg + 1) * span] = jnp.concatenate([re, im], axis=0).T
            lt[width:, seg * span:(seg + 1) * span] = jnp.concatenate([im, -re], axis=0).T

    def products(c, column, put):
        depth = 8 * blocks.shape[4]
        for n in range(0, NZ, 2):
            pair = [blocks[c, (n + k) * NY + column].reshape(depth, width) for k in range(2)]
            prod = jnp.dot(lt[...], jnp.concatenate(pair, axis=1), preferred_element_type=jnp.float32)
            prod = (prod * (2.0 / depth)).astype(jnp.bfloat16)
            for k in range(2):
                for h in range(2):
                    put(n + k, h, prod[h * width:(h + 1) * width, k * width:(k + 1) * width])

    def put_row(c, column):
        def put(n, h, value):
            at = pl.ds(pl.multiple_of((n * NY + column) * width, width), width)
            vout[c, h, :, at] = value
        return put

    def put_send(c, side):
        def put(n, h, value):
            vsend[c, side, n, h] = value
        return put

    def arrived(c):
        for d in (0, 2, 1, 3):
            for stage in range(2):
                y_copy(c, d, stage).wait_recv()
        for stage in range(2):
            b_copy(c, stage).wait_recv()

    def correlate(c):
        arrived(c)
        left_rows(c, z * NY + back(c))
        products(c, y, put_send(c, 0))
        v_copy(c, 0).start()
        left_rows(c, z * NY + fwd(c))
        products(c, back(c), put_send(c, 1))
        v_copy(c, 1).start()
        left_rows(c, i)
        for column in (y, back(c)):
            products(c, column, put_row(c, column))

    def collect(c):
        for side in range(2):
            v_copy(c, side).wait_recv()
            column = (fwd(c), lax.rem(y + 2, NY))[side]
            for n in range(NZ):
                for h in range(2):
                    put_row(c, column)(n, h, vin[c, side, n, h])
        pltpu.make_async_copy(vout.at[c], out_hbm.at[:, c], out_sem.at[c]).start()

    def channel(c):
        weights(c)
        filtered(c, 0, pairs)
        if c == 0:
            pl.semaphore_wait(barrier, len(peers) + GROUP * len(steps))
        finish(c)

    channel(0)
    channel(1)
    first_half(0)
    channel(2)
    second_half(0)
    spread(0, 0)
    first_half(1)
    channel(3)
    spread(0, 1)
    second_half(1)
    spread(1, 0)
    first_half(2)
    spread(1, 1)
    second_half(2)
    spread(2, 0)
    first_half(3)
    correlate(0)
    spread(2, 1)
    second_half(3)
    spread(3, 0)
    correlate(1)
    spread(3, 1)
    collect(0)
    correlate(2)
    collect(1)
    correlate(3)
    collect(2)
    collect(3)
    for c in range(CH_DEV):
        for d in range(1, GROUP):
            turn_copy(c, d).wait_send()
        for d in range(GROUP):
            mid_copy(c, d).wait_send()

        @pl.when(core == 0)
        def _():
            for member in range(GROUP):
                ahead_copy(c, member).wait_send()

        for side in range(2):
            cross_copy(c, side).wait_send()
        for stage in range(2):
            for d in range(1, NZ):
                z_each(d, lambda: z_copy(c, d, stage).wait_send())
            pl.when(inner)(lambda: zf_copy(c, stage).wait_send())
            b_copy(c, stage).wait_send()
            for d in range(NZ):
                y_copy(c, d, stage).wait_send()
        for side in range(2):
            v_copy(c, side).wait_send()
        pltpu.make_async_copy(vout.at[c], out_hbm.at[:, c], out_sem.at[c]).wait()


def on_device(samples, filter_taps):
    ntaps, nch = filter_taps.shape
    width = samples.shape[2]
    frames = samples.shape[1] // nch
    total = frames * TM
    rows = 2 * TM
    local = samples.reshape(2, frames, nch, width)
    dma = pltpu.SemaphoreType.DMA
    return pl.pallas_call(
        kernel,
        out_shape=jax.ShapeDtypeStruct((2, CH_DEV, width, INP * width), jnp.bfloat16),
        in_specs=[
            pl.BlockSpec(memory_space=pltpu.HBM),
            pl.BlockSpec(memory_space=pltpu.VMEM),
            pl.BlockSpec(memory_space=pltpu.VMEM),
        ],
        out_specs=pl.BlockSpec(memory_space=pl.ANY),
        scratch_shapes=[
            pltpu.VMEM((2, frames, nch, width), jnp.bfloat16),
            pltpu.VMEM((ntaps * rows, 2 * nch), jnp.bfloat16),
            pltpu.VMEM((2 * frames * rows, width), jnp.float32),
            pltpu.VMEM((CH_DEV, GROUP, 2, 2, 2 * frames, width), jnp.bfloat16),
            pltpu.VMEM((CH_DEV, GROUP, 2, 2 * frames, width), jnp.bfloat16),
            pltpu.VMEM((CH_DEV, GROUP, 2, 2 * frames, width), jnp.bfloat16),
            pltpu.VMEM((CH_DEV, 4, 2, frames, width), jnp.bfloat16),
            pltpu.VMEM((CH_DEV, 4, 2, 2, frames, width), jnp.bfloat16),
            pltpu.VMEM((CH_DEV, 4, 2, 2, frames, width), jnp.bfloat16),
            pltpu.VMEM((CH_DEV, INP, 4, 2, total // 4, width), jnp.bfloat16),
            pltpu.VMEM((2 * width, 2 * total), jnp.bfloat16),
            pltpu.VMEM((CH_DEV, 2, width, INP * width), jnp.bfloat16),
            pltpu.VMEM((CH_DEV, 2, NZ, 2, width, width), jnp.bfloat16),
            pltpu.VMEM((CH_DEV, 2, NZ, 2, width, width), jnp.bfloat16),
            dma((frames // 2,)),
            dma((CH_DEV, GROUP)),
            dma((CH_DEV, GROUP)),
            dma((CH_DEV, GROUP)),
            dma((CH_DEV, GROUP)),
            dma((CH_DEV, GROUP)),
            dma((CH_DEV, 4)),
            dma((CH_DEV, 2)),
            dma((CH_DEV, 2)),
            dma((CH_DEV, NZ, 2)),
            dma((CH_DEV, NZ, 2)),
            dma((CH_DEV, 2)),
            dma((CH_DEV, NZ, 2)),
            dma((CH_DEV, NZ, 2)),
            dma((CH_DEV, 2)),
            dma((CH_DEV, 2)),
            dma((CH_DEV, 2)),
            dma((CH_DEV, 2)),
            dma((CH_DEV,)),
        ],
        compiler_params=pltpu.CompilerParams(
            collective_id=0, has_side_effects=True, vmem_limit_bytes=54 * 1024 * 1024),
        name="correlator",
    )(local, filter_taps, jnp.asarray(trig_table(nch)))


def solution(mesh):
    in_specs = (P(None, "tm", "input"), P())
    out_specs = P(None, "tm", "input", None)
    return jax.shard_map(
        on_device, mesh=mesh, in_specs=in_specs, out_specs=out_specs, check_vma=False
    )
```

time: 135 us -> 112 us (0.83)
  the two profiles are of different devices: /device:TPU:96 before, /device:TPU:2 now
where the time goes in v2:
time: 112 us
  Pallas kernels  107 us (96%)
  local copies, waits for them, and re-layouts  4.79 us (4%)
    pallas_call x1, Pallas kernels, on_device(): pl.pallas_call(kernel, out_shape=jax.ShapeDtypeStruct((2, CH_DEV, width,...  107 us
    unnamed x1, local copies, waits for them, and re-layouts  4.79 us

profile of v2, /device:TPU:2, one launch (start us, length us, event | category | flops | bytes accessed | tf_op | source)
XLA Modules:
  0.0 111.6 jit_solution(15660040629219155084)
XLA Ops:
  0.0 106.8 %correlator.1 = bf16[2,4,128,2048]{3,2,1,0:T(8,128)(2,1)} custom-call(bf16[2,16,1024,128]{3,2,1,0:T(8,128)(2,1)} %bitcast.1, f32[16,1024]{1,0:T(8,128)} %taps_ref.1, f32[2,4,16,1024]{3,2,1,0:T(8,128)} %constant.2.clone.trig_ref), custom_call_target="tpu_custom_call" | custom-call | tf_op jit(solution)/shard_map/correlator/pallas_call | solution.py:400
  106.8 4.8 %copy.5 = bf16[2,4,128,2048]{3,2,1,0:T(8,128)(2,1)} copy(bf16[2,4,128,2048]{3,2,1,0:T(8,128)(2,1)} %correlator.1) | data formatting | bytes 8388608

commit v3 on v2

--- a/solution.py
+++ b/solution.py
@@ -25,9 +25,9 @@
     return np.stack([np.cos(theta) * scale, np.sin(theta) * scale]).astype(np.float32)
 
 
-def kernel(x_hbm, taps_ref, trig_ref, out_hbm, xv, ghi, acc, part, recv, mid, ahead, merged, crossed, blocks, lt, vout, vsend, vin,
-           x_sem, turn_send, turn_recv, mid_send, mid_recv, ahead_send, ahead_recv, cross_send, cross_recv,
-           z_send, z_recv, zf_send, y_send, y_recv, b_send, b_recv, v_send, v_recv, out_sem):
+def kernel(x_hbm, taps_ref, trig_ref, out_hbm, xv, ghi, acc, part, recv, ahead, far, blocks, lt, vout, vsend, vin,
+           x_sem, turn_send, turn_recv, ahead_send, ahead_recv,
+           z_send, z_recv, g_send, g_recv, t_send, y_send, y_recv, b_send, b_recv, v_send, v_recv, out_sem):
     t = lax.axis_index("tm")
     i = lax.axis_index("input")
     x = t // 4
@@ -38,7 +38,6 @@
     y = lax.rem(i, NY)
     q = 2 * x + core
     ring = zhi * NZ + z
-    toward = jnp.where(x == 0, 1, -1)
     up = lax.rem(y + 1, NY)
     down = lax.rem(y + NY - 1, NY)
     ntaps, nch = taps_ref.shape
@@ -69,17 +68,15 @@
 
     barrier = pltpu.get_barrier_semaphore()
     peers = [at_group(lax.rem(q + d, GROUP)) for d in range(1, GROUP)]
-    peers += [at_ring(q, ring + step) for step in (3, -3)]
+    peers += [at_ring(q, other * NZ + lax.rem(z + d, NZ)) for d in range(1, NZ)]
     peers += [at_z(lax.rem(z + d, NZ)) for d in range(1, NZ)]
     peers += [at_y(up), at_y(down)]
     for peer in peers:
         pl.semaphore_signal(barrier, inc=1, device_id=peer, device_id_type=MESH)
-    steps = (1, -1, NZ)
 
     @pl.loop(0, GROUP)
     def _(member):
-        for step in steps:
-            pl.semaphore_signal(barrier, inc=1, device_id=at_ring(member, ring + step), device_id_type=MESH)
+        pl.semaphore_signal(barrier, inc=1, device_id=at_ring(member, ring + NZ), device_id_type=MESH)
 
     def weights(c):
         cosine = trig_ref[0, c]
@@ -113,35 +110,21 @@
     def turn_copy(c, d):
         member = lax.rem(q + d, GROUP)
         return pltpu.make_async_remote_copy(
-            src_ref=part.at[c, member, zhi], dst_ref=recv.at[c, q],
+            src_ref=part.at[c, member], dst_ref=recv.at[c, q],
             send_sem=turn_send.at[c, d], recv_sem=turn_recv.at[c, d],
             device_id=at_group(member), device_id_type=MESH)
 
-    def mid_copy(c, d):
-        member = lax.rem(q + d, GROUP)
-        return pltpu.make_async_remote_copy(
-            src_ref=part.at[c, member, other], dst_ref=mid.at[c, q],
-            send_sem=mid_send.at[c, d], recv_sem=mid_recv.at[c, d],
-            device_id=at_ring(member, ring + toward), device_id_type=MESH)
-
     def ahead_copy(c, member):
         return pltpu.make_async_remote_copy(
-            src_ref=part.at[c, member, other, :, pl.ds(0, frames)], dst_ref=ahead.at[c, x],
+            src_ref=part.at[c, member, :, :, pl.ds(0, frames)], dst_ref=ahead.at[c, x],
             send_sem=ahead_send.at[c, member], recv_sem=ahead_recv.at[c, x],
             device_id=at_ring(member, ring + NZ), device_id_type=MESH)
 
     def ahead_arrival(c, k):
         return pltpu.make_async_remote_copy(
-            src_ref=part.at[c, 0, 0, :, pl.ds(0, frames)], dst_ref=ahead.at[c, k],
+            src_ref=part.at[c, 0, :, :, pl.ds(0, frames)], dst_ref=ahead.at[c, k],
             send_sem=ahead_send.at[c, 0], recv_sem=ahead_recv.at[c, k],
             device_id=at_ring(q, ring + NZ), device_id_type=MESH)
-
-    def cross_copy(c, side):
-        sl = (pl.ds(0, 1), pl.ds(1, 3))[side]
-        return pltpu.make_async_remote_copy(
-            src_ref=merged.at[c, sl], dst_ref=crossed.at[c, sl],
-            send_sem=cross_send.at[c, side], recv_sem=cross_recv.at[c, side],
-            device_id=at_ring(q, ring + (3, -3)[side]), device_id_type=MESH)
 
     def finish(c):
         for h in range(2):
@@ -149,48 +132,45 @@
                 r = h * TM + owner
                 member, side = (owner // 4) * 2 + owner % 2, (owner // 2) % 2
                 part[c, member, side, h] = acc[pl.ds(r, rows, stride=rows), :].astype(jnp.bfloat16)
-        recv[c, q] = part[c, q, zhi]
+        recv[c, q] = part[c, q]
 
         @pl.when(core == 0)
         def _():
             for member in range(GROUP):
                 ahead_copy(c, member).start()
 
-        for d in range(GROUP):
-            mid_copy(c, d).start()
         for d in range(1, GROUP):
             turn_copy(c, d).start()
 
-    def segments(c, slot, stage):
-        return blocks.at[c, slot, pl.ds(2 * stage, 2)]
-
-    def z_copy(c, d, stage):
-        ref = segments(c, i, stage)
+    def segments(c, slot, group):
+        return blocks.at[c, slot, pl.ds(2 * group, 2)]
+
+    def near_copy(c, d):
+        ref = segments(c, i, zhi)
         return pltpu.make_async_remote_copy(
             src_ref=ref, dst_ref=ref,
-            send_sem=z_send.at[c, d, stage], recv_sem=z_recv.at[c, d, stage],
+            send_sem=z_send.at[c, d], recv_sem=z_recv.at[c, d],
             device_id=at_z(lax.rem(z + d, NZ)), device_id_type=MESH)
 
-    def z_far(d):
-        return (z == 3) if d == 1 else (z == 0) if d == 3 else None
-
-    def z_each(d, act):
-        far = z_far(d)
-        if far is None:
-            act()
-        else:
-            pl.when(jnp.logical_not(far))(act)
-
-    inner = jnp.logical_or(z == 1, z == 2)
-
-    def zf_copy(c, stage):
-        source = lax.rem(z + 2, NZ)
-        target = jnp.where(z == 1, 0, 3)
-        ref = segments(c, source * NY + y, stage)
+    def far_copy(c, d):
+        return pltpu.make_async_remote_copy(
+            src_ref=far.at[c], dst_ref=segments(c, i, zhi),
+            send_sem=g_send.at[c, d], recv_sem=g_recv.at[c, z],
+            device_id=at_ring(q, other * NZ + lax.rem(z + d, NZ)), device_id_type=MESH)
+
+    def far_arrival(c, source):
+        ref = segments(c, source * NY + y, other)
         return pltpu.make_async_remote_copy(
             src_ref=ref, dst_ref=ref,
-            send_sem=zf_send.at[c, stage], recv_sem=z_recv.at[c, jnp.where(z == 1, 1, 3), stage],
-            device_id=at_z(target), device_id_type=MESH)
+            send_sem=g_send.at[c, 0], recv_sem=g_recv.at[c, source],
+            device_id=at_z(lax.rem(z + 1, NZ)), device_id_type=MESH)
+
+    def tie_copy(c, source, slot):
+        ref = segments(c, source * NY + y, other)
+        return pltpu.make_async_remote_copy(
+            src_ref=ref, dst_ref=ref,
+            send_sem=t_send.at[c, slot], recv_sem=g_recv.at[c, source],
+            device_id=at_z(source), device_id_type=MESH)
 
     def fwd(c):
         return (up, down)[c % 2]
@@ -199,14 +179,14 @@
         return (down, up)[c % 2]
 
     def y_copy(c, d, stage):
-        ref = segments(c, lax.rem(z + NZ - d, NZ) * NY + y, stage)
+        ref = segments(c, lax.rem(z + NZ - d, NZ) * NY + y, (zhi, other)[stage])
         return pltpu.make_async_remote_copy(
             src_ref=ref, dst_ref=ref,
             send_sem=y_send.at[c, d, stage], recv_sem=y_recv.at[c, d, stage],
             device_id=at_y(fwd(c)), device_id_type=MESH)
 
     def b_copy(c, stage):
-        ref = segments(c, i, stage)
+        ref = segments(c, i, (zhi, other)[stage])
         return pltpu.make_async_remote_copy(
             src_ref=ref, dst_ref=ref,
             send_sem=b_send.at[c, stage], recv_sem=b_recv.at[c, stage],
@@ -221,56 +201,54 @@
     def total(a, b):
         return (a.astype(jnp.float32) + b.astype(jnp.float32)).astype(jnp.bfloat16)
 
-    def send_own(c, stage):
-        y_copy(c, 0, stage).start()
-        b_copy(c, stage).start()
-        for d in (2, 1, 3):
-            z_each(d, lambda: z_copy(c, d, stage).start())
-
-    def first_half(c):
-        for d in range(GROUP):
-            mid_copy(c, d).wait_recv()
-        for k in range(4):
-            for h in range(2):
-                merged[c, k, 0, h] = total(mid[c, 2 * k, h, frames:, :], mid[c, 2 * k + 1, h, :frames, :])
-                merged[c, k, 1, h] = mid[c, 2 * k + 1, h, frames:, :]
-        for side in range(2):
-            cross_copy(c, side).start()
+    def merge(c):
         for d in range(1, GROUP):
             turn_copy(c, d).wait_recv()
         for k in range(4):
             ahead_arrival(c, k).wait_recv()
-        for k in range(4):
-            there = jnp.minimum(k + zhi, 3)
-            for h in range(2):
+        for group in (other, zhi):
+            for k in range(4):
+                there = jnp.minimum(k + zhi, 3)
                 at = slice(k * frames, (k + 1) * frames)
-                blocks[c, i, 0, h, at] = total(recv[c, 2 * k, h, frames:, :], recv[c, 2 * k + 1, h, :frames, :])
-                rest = ahead[c, there, h].astype(jnp.float32)
-                if k == 3:
-                    rest = jnp.where(zhi == 0, rest, 0.0)
-                blocks[c, i, 1, h, at] = total(recv[c, 2 * k + 1, h, frames:, :], rest)
-        send_own(c, 0)
-
-    def second_half(c):
-        for side in range(2):
-            cross_copy(c, side).wait_recv()
-        for k in range(4):
-            here = jnp.minimum(k + other, 3)
-            for h in range(2):
-                at = slice(k * frames, (k + 1) * frames)
-                blocks[c, i, 2, h, at] = crossed[c, k, 0, h]
-                rest = recv[c, 2 * here, h, :frames, :].astype(jnp.float32)
-                if k == 3:
-                    rest = jnp.where(zhi == 1, rest, 0.0)
-                blocks[c, i, 3, h, at] = total(crossed[c, k, 1, h], rest)
-        send_own(c, 1)
-
-    def spread(c, stage):
+                for h in range(2):
+                    first = total(recv[c, 2 * k, group, h, frames:, :], recv[c, 2 * k + 1, group, h, :frames, :])
+                    rest = ahead[c, there, group, h].astype(jnp.float32)
+                    if k == 3:
+                        rest = jnp.where(zhi == 0, rest, 0.0)
+                    second = total(recv[c, 2 * k + 1, group, h, frames:, :], rest)
+                    if group is other:
+                        far[c, 0, h, at] = first
+                        far[c, 1, h, at] = second
+                    else:
+                        blocks[c, i, 2 * zhi, h, at] = first
+                        blocks[c, i, 2 * zhi + 1, h, at] = second
+            if group is other:
+                for d in (1, 3, 2):
+                    far_copy(c, d).start()
+        y_copy(c, 0, 0).start()
+        b_copy(c, 0).start()
         for d in (2, 1, 3):
-            z_copy(c, d, stage).wait_recv()
-            if d == 2:
-                pl.when(inner)(lambda: zf_copy(c, stage).start())
-            y_copy(c, d, stage).start()
+            near_copy(c, d).start()
+
+    def spread_near(c):
+        for d in (2, 1, 3):
+            near_copy(c, d).wait_recv()
+            y_copy(c, d, 0).start()
+
+    def spread_far(c):
+        for d in (1, 3, 2):
+            source = lax.rem(z + NZ - d, NZ)
+            far_arrival(c, source).wait_recv()
+            if d == 1:
+                pl.when(z >= 1)(lambda: tie_copy(c, z - 1, 0).start())
+            if d == 3:
+                pl.when(z == 2)(lambda: tie_copy(c, 3, 1).start())
+            y_copy(c, d, 1).start()
+
+    def spread_tie(c):
+        far_arrival(c, z).wait_recv()
+        y_copy(c, 0, 1).start()
+        b_copy(c, 1).start()
 
     def left_rows(c, slot):
         span = 2 * blocks.shape[4]
@@ -333,31 +311,31 @@
         weights(c)
         filtered(c, 0, pairs)
         if c == 0:
-            pl.semaphore_wait(barrier, len(peers) + GROUP * len(steps))
+            pl.semaphore_wait(barrier, len(peers) + GROUP)
         finish(c)
 
     channel(0)
     channel(1)
-    first_half(0)
+    merge(0)
     channel(2)
-    second_half(0)
-    spread(0, 0)
-    first_half(1)
+    spread_near(0)
+    spread_far(0)
+    merge(1)
     channel(3)
-    spread(0, 1)
-    second_half(1)
-    spread(1, 0)
-    first_half(2)
-    spread(1, 1)
-    second_half(2)
-    spread(2, 0)
-    first_half(3)
+    spread_tie(0)
+    spread_near(1)
+    spread_far(1)
+    merge(2)
+    spread_tie(1)
     correlate(0)
-    spread(2, 1)
-    second_half(3)
-    spread(3, 0)
+    spread_near(2)
+    spread_far(2)
+    merge(3)
+    spread_tie(2)
     correlate(1)
-    spread(3, 1)
+    spread_near(3)
+    spread_far(3)
+    spread_tie(3)
     collect(0)
     correlate(2)
     collect(1)
@@ -367,20 +345,18 @@
     for c in range(CH_DEV):
         for d in range(1, GROUP):
             turn_copy(c, d).wait_send()
-        for d in range(GROUP):
-            mid_copy(c, d).wait_send()
 
         @pl.when(core == 0)
         def _():
             for member in range(GROUP):
                 ahead_copy(c, member).wait_send()
 
-        for side in range(2):
-            cross_copy(c, side).wait_send()
+        for d in range(1, NZ):
+            near_copy(c, d).wait_send()
+            far_copy(c, d).wait_send()
+        pl.when(z >= 1)(lambda: tie_copy(c, z - 1, 0).wait_send())
+        pl.when(z == 2)(lambda: tie_copy(c, 3, 1).wait_send())
         for stage in range(2):
-            for d in range(1, NZ):
-                z_each(d, lambda: z_copy(c, d, stage).wait_send())
-            pl.when(inner)(lambda: zf_copy(c, stage).wait_send())
             b_copy(c, stage).wait_send()
             for d in range(NZ):
                 y_copy(c, d, stage).wait_send()
@@ -411,11 +387,9 @@
             pltpu.VMEM((ntaps * rows, 2 * nch), jnp.bfloat16),
             pltpu.VMEM((2 * frames * rows, width), jnp.float32),
             pltpu.VMEM((CH_DEV, GROUP, 2, 2, 2 * frames, width), jnp.bfloat16),
-            pltpu.VMEM((CH_DEV, GROUP, 2, 2 * frames, width), jnp.bfloat16),
-            pltpu.VMEM((CH_DEV, GROUP, 2, 2 * frames, width), jnp.bfloat16),
-            pltpu.VMEM((CH_DEV, 4, 2, frames, width), jnp.bfloat16),
+            pltpu.VMEM((CH_DEV, GROUP, 2, 2, 2 * frames, width), jnp.bfloat16),
             pltpu.VMEM((CH_DEV, 4, 2, 2, frames, width), jnp.bfloat16),
-            pltpu.VMEM((CH_DEV, 4, 2, 2, frames, width), jnp.bfloat16),
+            pltpu.VMEM((CH_DEV, 2, 2, total // 4, width), jnp.bfloat16),
             pltpu.VMEM((CH_DEV, INP, 4, 2, total // 4, width), jnp.bfloat16),
             pltpu.VMEM((2 * width, 2 * total), jnp.bfloat16),
             pltpu.VMEM((CH_DEV, 2, width, INP * width), jnp.bfloat16),
@@ -425,13 +399,11 @@
             dma((CH_DEV, GROUP)),
             dma((CH_DEV, GROUP)),
             dma((CH_DEV, GROUP)),
-            dma((CH_DEV, GROUP)),
-            dma((CH_DEV, GROUP)),
             dma((CH_DEV, 4)),
-            dma((CH_DEV, 2)),
-            dma((CH_DEV, 2)),
-            dma((CH_DEV, NZ, 2)),
-            dma((CH_DEV, NZ, 2)),
+            dma((CH_DEV, NZ)),
+            dma((CH_DEV, NZ)),
+            dma((CH_DEV, NZ)),
+            dma((CH_DEV, NZ)),
             dma((CH_DEV, 2)),
             dma((CH_DEV, NZ, 2)),
             dma((CH_DEV, NZ, 2)),
@@ -442,7 +414,7 @@
             dma((CH_DEV,)),
         ],
         compiler_params=pltpu.CompilerParams(
-            collective_id=0, has_side_effects=True, vmem_limit_bytes=54 * 1024 * 1024),
+            collective_id=0, has_side_effects=True, vmem_limit_bytes=48 * 1024 * 1024),
         name="correlator",
     )(local, filter_taps, jnp.asarray(trig_table(nch)))
 

time: 112 us -> 99.2 us (0.89); the launches traced: 112 us -> 97.6 us
  Pallas kernels: 107 us -> 93.7 us
    pallas_call x1, Pallas kernels: 107 us -> 93.7 us  [on_device(): pl.pallas_call(kernel, out_shape=jax.ShapeDtypeStruct((2, CH_DEV, width,...]
    unnamed x1 -> x5, local copies, waits for them, and re-layouts: 4.79 us -> 3.9 us
where the time goes in v3:
time: 99.2 us; the launch traced here: 97.6 us
  Pallas kernels  93.7 us (94%)
  local copies, waits for them, and re-layouts  3.9 us (4%)
    pallas_call x1, Pallas kernels, on_device(): pl.pallas_call(kernel, out_shape=jax.ShapeDtypeStruct((2, CH_DEV, width,...  93.7 us
    unnamed x5, local copies, waits for them, and re-layouts  3.9 us

profile of v3, /device:TPU:2, one launch (start us, length us, event | category | flops | bytes accessed | tf_op | source)
XLA Modules:
  0.0 97.6 jit_solution(11819543101248674038)
XLA Ops:
  0.0 0.0 copy-start
  0.0 1.0 %copy-done = f32[2,4,16,1024]{3,2,1,0:T(8,128)S(1)} copy-done((f32[2,4,16,1024]{3,2,1,0:T(8,128)S(1)}, f32[2,4,16,1024]{3,2,1,0:T(8,128)}, u32[]{:S(2)}) %copy-start) | copy-done | bytes 524312
  1.0 0.0 copy-start.1
  1.0 0.8 copy-done.1
  1.9 93.7 %correlator.1 = bf16[2,4,128,2048]{3,2,1,0:T(8,128)(2,1)S(1)} custom-call(bf16[2,16,1024,128]{3,2,1,0:T(8,128)(2,1)} %bitcast.1, f32[16,1024]{1,0:T(8,128)S(1)} %copy-done.1, f32[2,4,16,1024]{3,2,1,0:T(8,128)S(1)} %copy-done), custom_call_target="tpu_custom_call" | custom-call | tf_op jit(solution)/shard_map/correlator/pallas_call | solution.py:376
  95.6 2.0 %copy.5 = bf16[2,4,128,2048]{3,2,1,0:T(8,128)(2,1)} copy(bf16[2,4,128,2048]{3,2,1,0:T(8,128)(2,1)S(1)} %correlator.1) | data formatting | bytes 8388608
Async XLA Ops:
  0.0 1.0 %copy-start = (f32[2,4,16,1024]{3,2,1,0:T(8,128)S(1)}, f32[2,4,16,1024]{3,2,1,0:T(8,128)}, u32[]{:S(2)}) copy-start(f32[2,4,16,1024]{3,2,1,0:T(8,128)} %constant.2.clone.trig_ref) | copy-start | bytes 1572868
  1.0 0.8 copy-start.1

commit v4 on v3

--- a/solution.py
+++ b/solution.py
@@ -14,6 +14,8 @@
 NY = 4
 NZ = 4
 INP = NY * NZ
+FWD = (0, 1, 3)
+BACK = (0, 2)
 GROUP = 8
 
 
@@ -185,16 +187,23 @@
             send_sem=y_send.at[c, d, stage], recv_sem=y_recv.at[c, d, stage],
             device_id=at_y(fwd(c)), device_id_type=MESH)
 
-    def b_copy(c, stage):
-        ref = segments(c, i, (zhi, other)[stage])
+    def b_copy(c, d, stage):
+        ref = segments(c, lax.rem(z + NZ - d, NZ) * NY + y, (zhi, other)[stage])
         return pltpu.make_async_remote_copy(
             src_ref=ref, dst_ref=ref,
-            send_sem=b_send.at[c, stage], recv_sem=b_recv.at[c, stage],
+            send_sem=b_send.at[c, d, stage], recv_sem=b_recv.at[c, d, stage],
             device_id=at_y(back(c)), device_id_type=MESH)
 
+    def ring_start(c, d, stage):
+        if d in FWD:
+            y_copy(c, d, stage).start()
+        if d in BACK:
+            b_copy(c, d, stage).start()
+
     def v_copy(c, side):
-        return pltpu.make_async_remote_copy(
-            src_ref=vsend.at[c, side], dst_ref=vin.at[c, side],
+        sl = pl.ds(0, (4, 3)[side])
+        return pltpu.make_async_remote_copy(
+            src_ref=vsend.at[c, side, sl], dst_ref=vin.at[c, side, sl],
             send_sem=v_send.at[c, side], recv_sem=v_recv.at[c, side],
             device_id=at_y((back(c), fwd(c))[side]), device_id_type=MESH)
 
@@ -225,15 +234,14 @@
             if group is other:
                 for d in (1, 3, 2):
                     far_copy(c, d).start()
-        y_copy(c, 0, 0).start()
-        b_copy(c, 0).start()
+        ring_start(c, 0, 0)
         for d in (2, 1, 3):
             near_copy(c, d).start()
 
     def spread_near(c):
         for d in (2, 1, 3):
             near_copy(c, d).wait_recv()
-            y_copy(c, d, 0).start()
+            ring_start(c, d, 0)
 
     def spread_far(c):
         for d in (1, 3, 2):
@@ -243,12 +251,11 @@
                 pl.when(z >= 1)(lambda: tie_copy(c, z - 1, 0).start())
             if d == 3:
                 pl.when(z == 2)(lambda: tie_copy(c, 3, 1).start())
-            y_copy(c, d, 1).start()
+            ring_start(c, d, 1)
 
     def spread_tie(c):
         far_arrival(c, z).wait_recv()
-        y_copy(c, 0, 1).start()
-        b_copy(c, 1).start()
+        ring_start(c, 0, 1)
 
     def left_rows(c, slot):
         span = 2 * blocks.shape[4]
@@ -258,53 +265,58 @@
             lt[:width, seg * span:(seg + 1) * span] = jnp.concatenate([re, im], axis=0).T
             lt[width:, seg * span:(seg + 1) * span] = jnp.concatenate([im, -re], axis=0).T
 
-    def products(c, column, put):
+    def slot_of(column, d):
+        return lax.rem(z + NZ - d, NZ) * NY + column
+
+    def products(c, wanted, put):
         depth = 8 * blocks.shape[4]
-        for n in range(0, NZ, 2):
-            pair = [blocks[c, (n + k) * NY + column].reshape(depth, width) for k in range(2)]
-            prod = jnp.dot(lt[...], jnp.concatenate(pair, axis=1), preferred_element_type=jnp.float32)
+        for n in range(0, len(wanted), 2):
+            pair = wanted[n:n + 2]
+            right = [blocks[c, slot_of(*where)].reshape(depth, width) for where in pair]
+            prod = jnp.dot(lt[...], jnp.concatenate(right, axis=1), preferred_element_type=jnp.float32)
             prod = (prod * (2.0 / depth)).astype(jnp.bfloat16)
-            for k in range(2):
+            for k, where in enumerate(pair):
                 for h in range(2):
-                    put(n + k, h, prod[h * width:(h + 1) * width, k * width:(k + 1) * width])
-
-    def put_row(c, column):
-        def put(n, h, value):
-            at = pl.ds(pl.multiple_of((n * NY + column) * width, width), width)
+                    put(n + k, where, h, prod[h * width:(h + 1) * width, k * width:(k + 1) * width])
+
+    def put_row(c):
+        def put(n, where, h, value):
+            at = pl.ds(pl.multiple_of(slot_of(*where) * width, width), width)
             vout[c, h, :, at] = value
         return put
 
     def put_send(c, side):
-        def put(n, h, value):
+        def put(n, where, h, value):
             vsend[c, side, n, h] = value
         return put
 
-    def arrived(c):
-        for d in (0, 2, 1, 3):
-            for stage in range(2):
-                y_copy(c, d, stage).wait_recv()
+    def correlate(c):
         for stage in range(2):
-            b_copy(c, stage).wait_recv()
-
-    def correlate(c):
-        arrived(c)
+            y_copy(c, 0, stage).wait_recv()
         left_rows(c, z * NY + back(c))
-        products(c, y, put_send(c, 0))
+        for stage in range(2):
+            for d in BACK:
+                b_copy(c, d, stage).wait_recv()
+        products(c, [(y, 1), (y, 3), (fwd(c), 0), (fwd(c), 2)], put_send(c, 0))
         v_copy(c, 0).start()
         left_rows(c, z * NY + fwd(c))
-        products(c, back(c), put_send(c, 1))
+        for stage in range(2):
+            for d in FWD[1:]:
+                y_copy(c, d, stage).wait_recv()
+        products(c, [(back(c), 1), (back(c), 3), (y, 2)], put_send(c, 1))
         v_copy(c, 1).start()
         left_rows(c, i)
-        for column in (y, back(c)):
-            products(c, column, put_row(c, column))
+        here = [(y, d) for d in range(NZ)] + [(back(c), d) for d in FWD] + [(fwd(c), d) for d in BACK]
+        products(c, here, put_row(c))
 
     def collect(c):
+        across = lax.rem(y + 2, NY)
         for side in range(2):
             v_copy(c, side).wait_recv()
-            column = (fwd(c), lax.rem(y + 2, NY))[side]
-            for n in range(NZ):
+            got = ([(fwd(c), 1), (fwd(c), 3), (across, 0), (across, 2)], [(across, 1), (across, 3), (back(c), 2)])[side]
+            for n, where in enumerate(got):
                 for h in range(2):
-                    put_row(c, column)(n, h, vin[c, side, n, h])
+                    put_row(c)(n, where, h, vin[c, side, n, h])
         pltpu.make_async_copy(vout.at[c], out_hbm.at[:, c], out_sem.at[c]).start()
 
     def channel(c):
@@ -357,9 +369,10 @@
         pl.when(z >= 1)(lambda: tie_copy(c, z - 1, 0).wait_send())
         pl.when(z == 2)(lambda: tie_copy(c, 3, 1).wait_send())
         for stage in range(2):
-            b_copy(c, stage).wait_send()
-            for d in range(NZ):
+            for d in FWD:
                 y_copy(c, d, stage).wait_send()
+            for d in BACK:
+                b_copy(c, d, stage).wait_send()
         for side in range(2):
             v_copy(c, side).wait_send()
         pltpu.make_async_copy(vout.at[c], out_hbm.at[:, c], out_sem.at[c]).wait()
@@ -407,8 +420,8 @@
             dma((CH_DEV, 2)),
             dma((CH_DEV, NZ, 2)),
             dma((CH_DEV, NZ, 2)),
-            dma((CH_DEV, 2)),
-            dma((CH_DEV, 2)),
+            dma((CH_DEV, NZ, 2)),
+            dma((CH_DEV, NZ, 2)),
             dma((CH_DEV, 2)),
             dma((CH_DEV, 2)),
             dma((CH_DEV,)),

time: 99.2 us -> 95.7 us (0.965); the launches traced: 97.6 us -> 95.2 us
  Pallas kernels: 93.7 us -> 91.3 us
    pallas_call x1, Pallas kernels: 93.7 us -> 91.3 us  [on_device(): pl.pallas_call(kernel, out_shape=jax.ShapeDtypeStruct((2, CH_DEV, width,...]
where the time goes in v4:
time: 95.7 us; the launch traced here: 95.2 us
  Pallas kernels  91.3 us (95%)
  local copies, waits for them, and re-layouts  3.9 us (4%)
    pallas_call x1, Pallas kernels, on_device(): pl.pallas_call(kernel, out_shape=jax.ShapeDtypeStruct((2, CH_DEV, width,...  91.3 us
    unnamed x5, local copies, waits for them, and re-layouts  3.9 us

profile of v4, /device:TPU:2, one launch (start us, length us, event | category | flops | bytes accessed | tf_op | source)
XLA Modules:
  0.0 95.2 jit_solution(8664898625335382286)
XLA Ops:
  0.0 0.0 copy-start
  0.0 1.0 %copy-done = f32[2,4,16,1024]{3,2,1,0:T(8,128)S(1)} copy-done((f32[2,4,16,1024]{3,2,1,0:T(8,128)S(1)}, f32[2,4,16,1024]{3,2,1,0:T(8,128)}, u32[]{:S(2)}) %copy-start) | copy-done | bytes 524312
  1.0 0.0 copy-start.1
  1.0 0.8 copy-done.1
  1.9 91.3 %correlator.1 = bf16[2,4,128,2048]{3,2,1,0:T(8,128)(2,1)S(1)} custom-call(bf16[2,16,1024,128]{3,2,1,0:T(8,128)(2,1)} %bitcast.1, f32[16,1024]{1,0:T(8,128)S(1)} %copy-done.1, f32[2,4,16,1024]{3,2,1,0:T(8,128)S(1)} %copy-done), custom_call_target="tpu_custom_call" | custom-call | tf_op jit(solution)/shard_map/correlator/pallas_call | solution.py:389
  93.2 2.0 %copy.5 = bf16[2,4,128,2048]{3,2,1,0:T(8,128)(2,1)} copy(bf16[2,4,128,2048]{3,2,1,0:T(8,128)(2,1)S(1)} %correlator.1) | data formatting | bytes 8388608
Async XLA Ops:
  0.0 1.0 %copy-start = (f32[2,4,16,1024]{3,2,1,0:T(8,128)S(1)}, f32[2,4,16,1024]{3,2,1,0:T(8,128)}, u32[]{:S(2)}) copy-start(f32[2,4,16,1024]{3,2,1,0:T(8,128)} %constant.2.clone.trig_ref) | copy-start | bytes 1572868
  1.0 0.8 copy-start.1
